TPU v7x, 128 devices: a whole 4x4x4 slice. The times are simulated.
128 devices in a mesh: replica: 32 (over y, x, z_lo), tensor: 4 (over z_hi, core).
Axes of the slice: x: 4, y: 4, z: 4 (z_hi: 2, z_lo: 2; z = z_hi * 2 + z_lo), core: 2. Of those that a mesh axis runs over, the one named last changes fastest.
Arguments:
- weight: bfloat16 [32, 4096, 2048], P('replica', None, 'tensor'), may hold values from -0.09375 to 0.09375
- momentum: bfloat16 [32, 4096, 2048], P('replica', None, 'tensor'), may hold values from -24 to 24
- inputs: bfloat16 [2, 16384, 4096], P(None, ('replica', 'tensor')), may hold values from -6 to 6
- out_grads: bfloat16 [2, 16384, 2048], P(None, 'replica', 'tensor'), may hold values from -6 to 6
Outputs:
- new_weight: bfloat16 [32, 4096, 2048], P('replica', None, 'tensor')
- new_momentum: bfloat16 [32, 4096, 2048], P('replica', None, 'tensor')
- input_grad: bfloat16 [2, 16384, 4096], P(None, ('replica', 'tensor'))
All inputs are finite; a program needn't handle non-finite values.
Results may differ from a plain program's by a relative error of at most 0.014.
Values may be sent and summed in bfloat16 or wider, within the bound.
A program may use at most 128 MiB of HBM per device.

v0:
```python
import jax
import jax.numpy as jnp
from jax import lax
from jax.sharding import PartitionSpec as P

learn_rate = 0.001
mom_decay = 0.9


def in_blocks(shard, dim, devices):
    dims = shard.shape
    blocks = shard.reshape(*dims[:dim], devices, dims[dim] // devices, *dims[dim + 1 :])
    return jnp.moveaxis(blocks, dim, 0)


def sum_at_owner(shard, axis, dim):
    blocks = in_blocks(shard, dim, lax.axis_size(axis))
    arrived = lax.all_to_all(blocks, axis, split_axis=0, concat_axis=0, tiled=True)
    return arrived.astype(jnp.float32).sum(axis=0)


def from_partner(block, axis, distance):
    count = lax.axis_size(axis)
    route = []
    for low in range(count):
        high = low | 1 << distance
        if high != low and high < count:
            route += [(low, high), (high, low)]
    return lax.ppermute(block, axis, route)


def silu_slope(pre):
    sigma = jax.nn.sigmoid(pre)
    return sigma * (1.0 + pre * (1.0 - sigma))


def input_partials(slope_grad, weight_now):
    partial_value = lax.dot_general(
        slope_grad, weight_now, (((1,), (1,)), ((), ())), preferred_element_type=jnp.float32
    )
    rounded = partial_value.astype(jnp.bfloat16)
    return sum_at_owner(rounded, "tensor", 0).astype(jnp.bfloat16)


def gossip_update(weight_now, moment_now, grad_w, step):
    moment_new = (mom_decay * moment_now.astype(jnp.float32) + grad_w).astype(jnp.bfloat16)
    stepped = (weight_now.astype(jnp.float32) - learn_rate * moment_new.astype(jnp.float32)).astype(
        jnp.bfloat16
    )
    other_weight, other_moment = from_partner((stepped, moment_new), "replica", step)
    averaged = ((stepped.astype(jnp.float32) + other_weight.astype(jnp.float32)) * 0.5).astype(
        jnp.bfloat16
    )
    moment_avg = ((moment_new.astype(jnp.float32) + other_moment.astype(jnp.float32)) * 0.5).astype(
        jnp.bfloat16
    )
    return (averaged, moment_avg)


def local(weight, momentum, inputs, out_grads):
    weight_now = weight[0]
    moment_now = momentum[0]
    grads_out = []
    for step in range(inputs.shape[0]):
        rows_here = inputs[step]
        gathered = lax.all_gather(rows_here, "tensor", axis=0, tiled=True)
        pre = jnp.dot(gathered, weight_now, preferred_element_type=jnp.float32)
        slope_grad = (out_grads[step].astype(jnp.float32) * silu_slope(pre)).astype(jnp.bfloat16)
        grad_w = lax.dot_general(
            gathered, slope_grad, (((0,), (0,)), ((), ())), preferred_element_type=jnp.float32
        )
        grads_out.append(input_partials(slope_grad, weight_now))
        next_weight, next_moment = gossip_update(weight_now, moment_now, grad_w, step)
        weight_now = next_weight
        moment_now = next_moment
    return (weight_now[None], moment_now[None], jnp.stack(grads_out))


def solution(mesh):
    return jax.shard_map(
        local,
        mesh=mesh,
        in_specs=(
            P("replica", None, "tensor"),
            P("replica", None, "tensor"),
            P(None, ("replica", "tensor"), None),
            P(None, "replica", "tensor"),
        ),
        out_specs=(
            P("replica", None, "tensor"),
            P("replica", None, "tensor"),
            P(None, ("replica", "tensor"), None),
        ),
        check_vma=False,
    )
```

profile of v0, /device:TPU:0, one launch (start us, length us, event | category | flops | bytes accessed | tf_op | source)
XLA Modules:
  0.0 492.5 jit_solution(18293548097176699641)
XLA Ops:
  7.2 0.0 all-gather.5.cloned.1.call-start
  7.2 3.2 fusion.48
  10.4 0.0 all-gather.5.cloned.1.call-update
  10.4 0.0 all-gather.7.cloned.1.call-start
  10.4 0.7 all-gather.7.cloned.1.call-update
  11.1 6.3 %copy.8 = bf16[1,4096,512]{1,2,0:T(8,128)(2,1)} copy(bf16[1,4096,512]{2,1,0:T(8,128)(2,1)} %param.5) | data formatting | bytes 8388608 | tf_op args[1]
  17.5 6.4 %copy.7 = bf16[1,4096,512]{1,2,0:T(8,128)(2,1)} copy(bf16[1,4096,512]{2,1,0:T(8,128)(2,1)} %param.4) | data formatting | bytes 8388608 | tf_op args[0]
  23.8 0.0 copy-start.5
  23.9 27.8 %all-gather.5.cloned.1.call-done = bf16[1,512,4096]{2,1,0:T(8,128)(2,1)} async-done(((bf16[1,128,4096]{2,1,0:T(8,128)(2,1)}), bf16[1,512,4096]{2,1,0:T(8,128)(2,1)}) %all-gather.5.cloned.1.call-update) | async-done | bytes 4194320 | tf_op jit(solution)/shard_map/all_gather | solution.py:66
  51.7 0.0 copy-start.1
  51.7 0.0 copy-start.2
  51.7 0.0 copy-start.4
  51.7 5.9 %fusion.13 = f32[512,512]{1,0:T(8,128)S(1)} fusion(bf16[1,4096,512]{2,1,0:T(8,128)(2,1)} %param.4, bf16[1,512,4096]{2,1,0:T(8,128)(2,1)} %all-gather.5.cloned.1.call-done), kind=kOutput, calls=%fused_computation.23 | convolution fusion | flops 2147483648 | bytes 9437184 | tf_op jit(solution)/shard_map/dot_general | solution.py:67
  57.6 0.0 copy-done.5
  57.6 0.0 copy-done.1
  57.6 0.0 copy-done.2
  57.6 1.2 copy-done.4
  58.8 6.5 %fusion.1 = (bf16[4096,512]{0,1:T(8,128)(2,1)}, bf16[4096,512]{0,1:T(8,128)(2,1)}) fusion(bf16[1,4096,512]{1,2,0:T(8,128)(2,1)S(1)} %copy-done.2, bf16[1,512,4096]{2,1,0:T(8,128)(2,1)S(1)} %copy-done.4, f32[512,512]{1,0:T(8,128)S(1)} %fusion.13, bf16[2,512,512]{2,1,0:T(8,128)(2,1)S(1)} %copy-done.5, bf16[1,4096,512]{1,2,0:T(8,128)(2,1)S(1)} %copy-done.1), kind=kOutput, calls=%fused_computation.5 | convolution fusion | flops 2168979456 | bytes 22544384 | tf_op jit(solution)/shard_map/dot_general | solution.py:69
  65.3 0.5 collective-permute-start
  65.8 1.5 collective-permute-start.1
  67.4 46.2 %all-gather.7.cloned.1.call-done = bf16[1,512,4096]{2,1,0:T(8,128)(2,1)} async-done(((bf16[1,128,4096]{2,1,0:T(8,128)(2,1)}), bf16[1,512,4096]{2,1,0:T(8,128)(2,1)}) %all-gather.7.cloned.1.call-update) | async-done | bytes 4194320 | tf_op jit(solution)/shard_map/all_gather | solution.py:66
  113.5 0.0 copy-start.3
  113.5 65.3 %collective-permute-done = bf16[4096,512]{0,1:T(8,128)(2,1)} collective-permute-done((bf16[4096,512]{0,1:T(8,128)(2,1)}, bf16[4096,512]{0,1:T(8,128)(2,1)}, u32[]{:S(2)}, u32[]{:S(2)}) %collective-permute-start) | collective-permute-done | bytes 4194336 | tf_op jit(solution)/shard_map/ppermute | solution.py:29
  178.8 7.0 %fusion.23 = f32[512,512]{1,0:T(8,128)S(1)} fusion(bf16[1,512,4096]{2,1,0:T(8,128)(2,1)} %all-gather.7.cloned.1.call-done, bf16[4096,512]{0,1:T(8,128)(2,1)} %collective-permute-done, bf16[4096,512]{0,1:T(8,128)(2,1)} %get-tuple-element.10), kind=kOutput, calls=%fused_computation.32 | convolution fusion | flops 2157969408 | bytes 13631488 | tf_op jit(solution)/shard_map/dot_general | solution.py:67
  185.9 0.0 copy-start
  185.9 82.6 %collective-permute-done.1 = bf16[4096,512]{0,1:T(8,128)(2,1)} collective-permute-done((bf16[4096,512]{0,1:T(8,128)(2,1)}, bf16[4096,512]{0,1:T(8,128)(2,1)}, u32[]{:S(2)}, u32[]{:S(2)}) %collective-permute-start.1) | collective-permute-done | bytes 4194336 | tf_op jit(solution)/shard_map/ppermute | solution.py:29
  268.5 0.0 copy-done.3
  268.5 9.2 %fusion.8 = bf16[4096,512]{0,1:T(8,128)(2,1)} fusion(bf16[4096,512]{0,1:T(8,128)(2,1)} %collective-permute-done.1, bf16[4096,512]{0,1:T(8,128)(2,1)} %get-tuple-element.11, bf16[1,512,4096]{2,1,0:T(8,128)(2,1)S(1)} %copy-done.3, f32[512,512]{1,0:T(8,128)S(1)} %fusion.23, bf16[2,512,512]{2,1,0:T(8,128)(2,1)S(1)} %copy-done.5), kind=kOutput, calls=%fused_computation.13 | convolution fusion | flops 2168979456 | bytes 18350080 | tf_op jit(solution)/shard_map/dot_general | solution.py:69
  277.7 1.5 collective-permute-start.3
  279.2 0.0 copy-done
  279.2 4.5 convolution_convert_fusion.1
  283.7 4.9 all-to-all-start
  288.6 81.8 %collective-permute-done.3 = bf16[4096,512]{0,1:T(8,128)(2,1)} collective-permute-done((bf16[4096,512]{0,1:T(8,128)(2,1)}, bf16[4096,512]{0,1:T(8,128)(2,1)}, u32[]{:S(2)}, u32[]{:S(2)}) %collective-permute-start.3) | collective-permute-done | bytes 4194336 | tf_op jit(solution)/shard_map/ppermute | solution.py:29
  370.4 9.9 %fusion.11 = (bf16[1,4096,512]{1,2,0:T(8,128)(2,1)}, bf16[4096,512]{0,1:T(8,128)(2,1)}) fusion(bf16[4096,512]{0,1:T(8,128)(2,1)} %collective-permute-done.3, bf16[4096,512]{0,1:T(8,128)(2,1)} %fusion.8, bf16[4096,512]{0,1:T(8,128)(2,1)} %collective-permute-done, bf16[4096,512]{0,1:T(8,128)(2,1)} %get-tuple-element.10), kind=kLoop, calls=%fused_computation.21 | loop fusion | flops 29360128 | bytes 25165824 | tf_op jit(solution)/shard_map/broadcast_in_dim | solution.py:76
  380.2 1.5 collective-permute-start.2
  381.7 8.2 %convolution_convert_fusion = bf16[512,4096]{1,0:T(8,128)(2,1)} fusion(f32[512,512]{1,0:T(8,128)S(1)} %fusion.23, bf16[2,512,512]{2,1,0:T(8,128)(2,1)S(1)} %copy-done.5, bf16[4096,512]{0,1:T(8,128)(2,1)} %collective-permute-done, bf16[4096,512]{0,1:T(8,128)(2,1)} %get-tuple-element.10), kind=kOutput, calls=%fused_computation.18 | convolution fusion | flops 2162688000 | bytes 14155776 | tf_op jit(solution)/shard_map/dot_general | solution.py:38
  389.9 0.0 all-to-all-done
  389.9 4.9 all-to-all-start.1
  394.8 3.1 reduce_sum.24
  397.8 46.7 %all-to-all-done.1 = bf16[4,128,4096]{2,1,0:T(8,128)(2,1)} async-done(((bf16[4,128,4096]{2,1,0:T(8,128)(2,1)}), bf16[4,128,4096]{2,1,0:T(8,128)(2,1)}, u32[]{:S(2)}, u32[]{:S(2)}) %all-to-all-start.1) | async-done | bytes 4194336 | tf_op jit(solution)/shard_map/all_to_all | solution.py:18
  444.5 3.1 reduce_sum.25
  447.6 1.5 pad_maximum_fusion
  449.1 6.4 %copy.11 = bf16[1,4096,512]{2,1,0:T(8,128)(2,1)} copy(bf16[1,4096,512]{1,2,0:T(8,128)(2,1)} %get-tuple-element.6) | data formatting | bytes 8388608
  455.5 16.6 %collective-permute-done.2 = bf16[4096,512]{0,1:T(8,128)(2,1)} collective-permute-done((bf16[4096,512]{0,1:T(8,128)(2,1)}, bf16[4096,512]{0,1:T(8,128)(2,1)}, u32[]{:S(2)}, u32[]{:S(2)}) %collective-permute-start.2) | collective-permute-done | bytes 4194336 | tf_op jit(solution)/shard_map/ppermute | solution.py:29
  472.0 7.2 %fusion.10 = bf16[1,4096,512]{1,2,0:T(8,128)(2,1)} fusion(bf16[4096,512]{0,1:T(8,128)(2,1)} %collective-permute-done.2, bf16[4096,512]{0,1:T(8,128)(2,1)} %get-tuple-element.7), kind=kLoop, calls=%fused_computation.20 | loop fusion | flops 10485760 | bytes 12582912 | tf_op jit(solution)/shard_map/broadcast_in_dim | solution.py:76
  479.2 6.4 %copy.10 = bf16[1,4096,512]{2,1,0:T(8,128)(2,1)} copy(bf16[1,4096,512]{1,2,0:T(8,128)(2,1)} %fusion.10) | data formatting | bytes 8388608
Async XLA Ops:
  7.2 44.5 %all-gather.5.cloned.1.call-start = ((), (), s32[]{:S(2)}) async-start(), calls=%async_computation.2 | async-start | bytes 5242880 | tf_op jit(solution)/shard_map/all_gather | solution.py:66
  10.4 103.1 %all-gather.7.cloned.1.call-start = ((), (), s32[]{:S(2)}) async-start(), calls=%async_computation.3 | async-start | bytes 5242880 | tf_op jit(solution)/shard_map/all_gather | solution.py:66
  23.8 33.8 %copy-start.5 = (bf16[2,512,512]{2,1,0:T(8,128)(2,1)S(1)}, bf16[2,512,512]{2,1,0:T(8,128)(2,1)}, u32[]{:S(2)}) copy-start(bf16[2,512,512]{2,1,0:T(8,128)(2,1)} %param.7) | copy-start | bytes 3145732
  51.7 5.9 %copy-start.1 = (bf16[1,4096,512]{1,2,0:T(8,128)(2,1)S(1)}, bf16[1,4096,512]{1,2,0:T(8,128)(2,1)}, u32[]{:S(2)}) copy-start(bf16[1,4096,512]{1,2,0:T(8,128)(2,1)} %copy.8) | copy-start | bytes 12582916
  51.7 5.9 %copy-start.2 = (bf16[1,4096,512]{1,2,0:T(8,128)(2,1)S(1)}, bf16[1,4096,512]{1,2,0:T(8,128)(2,1)}, u32[]{:S(2)}) copy-start(bf16[1,4096,512]{1,2,0:T(8,128)(2,1)} %copy.7) | copy-start | bytes 12582916
  51.7 7.1 %copy-start.4 = (bf16[1,512,4096]{2,1,0:T(8,128)(2,1)S(1)}, bf16[1,512,4096]{2,1,0:T(8,128)(2,1)}, u32[]{:S(2)}) copy-start(bf16[1,512,4096]{2,1,0:T(8,128)(2,1)} %all-gather.5.cloned.1.call-done) | copy-start | bytes 12582916
  65.3 113.5 %collective-permute-start = (bf16[4096,512]{0,1:T(8,128)(2,1)}, bf16[4096,512]{0,1:T(8,128)(2,1)}, u32[]{:S(2)}, u32[]{:S(2)}) collective-permute-start(bf16[4096,512]{0,1:T(8,128)(2,1)} %get-tuple-element.10), channel_id=1, source_target_pairs={{0,4},{4,0},{8,12},{12,8},{16,20},{20,16},{24,28},{28,24},{32,36},... | collective-permute-start | bytes 12582920 | tf_op jit(solution)/shard_map/ppermute | solution.py:29
  65.8 202.6 %collective-permute-start.1 = (bf16[4096,512]{0,1:T(8,128)(2,1)}, bf16[4096,512]{0,1:T(8,128)(2,1)}, u32[]{:S(2)}, u32[]{:S(2)}) collective-permute-start(bf16[4096,512]{0,1:T(8,128)(2,1)} %get-tuple-element.11), channel_id=1, source_target_pairs={{0,4},{4,0},{8,12},{12,8},{16,20},{20,16},{24,28},{28,24},{32,36},... | collective-permute-start | bytes 12582920 | tf_op jit(solution)/shard_map/ppermute | solution.py:29
  113.5 155.0 %copy-start.3 = (bf16[1,512,4096]{2,1,0:T(8,128)(2,1)S(1)}, bf16[1,512,4096]{2,1,0:T(8,128)(2,1)}, u32[]{:S(2)}) copy-start(bf16[1,512,4096]{2,1,0:T(8,128)(2,1)} %all-gather.7.cloned.1.call-done) | copy-start | bytes 12582916
  185.9 93.3 %copy-start = (bf16[1,4096,512]{2,1,0:T(8,128)(2,1)S(1)}, bf16[1,4096,512]{2,1,0:T(8,128)(2,1)}, u32[]{:S(2)}) copy-start(bf16[1,4096,512]{2,1,0:T(8,128)(2,1)} %param.4) | copy-start | bytes 12582916
  277.7 92.7 %collective-permute-start.3 = (bf16[4096,512]{0,1:T(8,128)(2,1)}, bf16[4096,512]{0,1:T(8,128)(2,1)}, u32[]{:S(2)}, u32[]{:S(2)}) collective-permute-start(bf16[4096,512]{0,1:T(8,128)(2,1)} %fusion.8), channel_id=1, source_target_pairs={{0,8},{8,0},{4,12},{12,4},{16,24},{24,16},{20,28},{28,20},{32,40},... | collective-permute-start | bytes 12582920 | tf_op jit(solution)/shard_map/ppermute | solution.py:29
  283.7 106.2 %all-to-all-start = ((bf16[4,128,4096]{2,1,0:T(8,128)(2,1)}), bf16[4,128,4096]{2,1,0:T(8,128)(2,1)}, u32[]{:S(2)}, u32[]{:S(2)}) async-start(bf16[4,128,4096]{2,1,0:T(8,128)(2,1)} %bitcast.66), calls=%async_computation | async-start | bytes 8388608 | tf_op jit(solution)/shard_map/all_to_all | solution.py:18
  380.2 91.8 %collective-permute-start.2 = (bf16[4096,512]{0,1:T(8,128)(2,1)}, bf16[4096,512]{0,1:T(8,128)(2,1)}, u32[]{:S(2)}, u32[]{:S(2)}) collective-permute-start(bf16[4096,512]{0,1:T(8,128)(2,1)} %get-tuple-element.7), channel_id=1, source_target_pairs={{0,8},{8,0},{4,12},{12,4},{16,24},{24,16},{20,28},{28,20},{32,40},... | collective-permute-start | bytes 12582920 | tf_op jit(solution)/shard_map/ppermute | solution.py:29
  389.9 54.6 %all-to-all-start.1 = ((bf16[4,128,4096]{2,1,0:T(8,128)(2,1)}), bf16[4,128,4096]{2,1,0:T(8,128)(2,1)}, u32[]{:S(2)}, u32[]{:S(2)}) async-start(bf16[4,128,4096]{2,1,0:T(8,128)(2,1)} %bitcast.67), calls=%async_computation.1 | async-start | bytes 8388608 | tf_op jit(solution)/shard_map/all_to_all | solution.py:18
Sparse Core Ops, SparseCore 0:
  10.5 41.1 all-gather.4
  53.9 59.5 all-gather.6
where the time goes:
time: 493 us; the launch traced here: 492 us
  waiting for transfers between devices  368 us (75%)
  matrix products  41.4 us (8%)
  local copies, waits for them, and re-layouts  29.8 us (6%)
  other arithmetic  24.7 us (5%)
  starting transfers between devices  14.8 us (3%)
  between operations  14.1 us (3%)
    ppermute x4, waiting for transfers between devices, from_partner(): return lax.ppermute(block, axis, route)  246 us
    all_gather x2, waiting for transfers between devices, local(): gathered = lax.all_gather(rows_here, 'tensor', axis=0, tiled=True)  74 us
    all_to_all x2, waiting for transfers between devices, sum_at_owner(): lax.all_to_all(blocks, axis, split_axis=0, concat_axis=0, tiled=True)  46.7 us
    unnamed x16, local copies, waits for them, and re-layouts  26.7 us
    broadcast_in_dim x2, other arithmetic, local(): return (weight_now[None], moment_now[None], jnp.stack(grads_out))  17 us
    dot_general x2, matrix products, local(): lax.dot_general(gathered, slope_grad, (((0,), (0,)), ((), ())), preferred...  15.7 us
    dot_general x2, matrix products, local(): pre = jnp.dot(gathered, weight_now, preferred_element_type=jnp.float32)  13 us
    dot_general x2, matrix products, input_partials(): lax.dot_general(slope_grad, weight_now, (((1,), (1,)), ((), ())), preferr...  12.7 us
  transfers between devices with their start and end apart: 8, of which 7 were waited for; matrix products, arithmetic and copies ran while one was open for 14% of the time, Pallas kernels for 0%

commit v1 on v0

--- a/solution.py
+++ b/solution.py
@@ -63,7 +63,10 @@
     grads_out = []
     for step in range(inputs.shape[0]):
         rows_here = inputs[step]
-        gathered = lax.all_gather(rows_here, "tensor", axis=0, tiled=True)
+        n_dev = lax.axis_size("tensor")
+        parts = jnp.stack([rows_here for _ in range(n_dev)])
+        parts = lax.all_to_all(parts, "tensor", split_axis=0, concat_axis=0)
+        gathered = jnp.concatenate(parts, axis=0)
         pre = jnp.dot(gathered, weight_now, preferred_element_type=jnp.float32)
         slope_grad = (out_grads[step].astype(jnp.float32) * silu_slope(pre)).astype(jnp.bfloat16)
         grad_w = lax.dot_general(

time: 493 us -> 519 us (1.053)
  blocking collectives: 0 us -> 225 us
  waiting for transfers between devices: 368 us -> 184 us
  between operations: 14.1 us -> 0.78 us
  matrix products: 41.4 us -> 32.3 us
  starting transfers between devices: 14.8 us -> 20 us
    all_to_all x0 -> x1, blocking collectives: none -> 225 us  [local(): parts = lax.all_to_all(parts, 'tensor', split_axis=0, concat_axis=0)]
    ppermute x4, waiting for transfers between devices: 246 us -> 101 us  [from_partner(): return lax.ppermute(block, axis, route)]
    all_gather x2 -> x0, waiting for transfers between devices: 74 us -> none  [local(): gathered = lax.all_gather(rows_here, 'tensor', axis=0, tiled=True)]
    all_to_all x0 -> x1, waiting for transfers between devices: none -> 37 us  [local(): parts = lax.all_to_all(parts, 'tensor', split_axis=0, concat_axis=0)]
    all_to_all x0 -> x1, starting transfers between devices: none -> 5.23 us  [local(): parts = lax.all_to_all(parts, 'tensor', split_axis=0, concat_axis=0)]
    unnamed x16 -> x20, local copies, waits for them, and re-layouts: 26.7 us -> 25.8 us
  transfers between devices with their start and end apart: 8 -> 7, of which waited for: 7 -> 4; matrix products, arithmetic and copies ran while one was open for 14% -> 9% of each run, Pallas kernels for 0% -> 0%
where the time goes in v1:
time: 519 us; the launch traced here: 518 us
  blocking collectives  225 us (43%)
  waiting for transfers between devices  184 us (35%)
  matrix products  32.3 us (6%)
  local copies, waits for them, and re-layouts  30.6 us (6%)
  other arithmetic  24.6 us (5%)
  starting transfers between devices  20 us (4%)
    all_to_all x1, blocking collectives, local(): parts = lax.all_to_all(parts, 'tensor', split_axis=0, concat_axis=0)  225 us
    ppermute x4, waiting for transfers between devices, from_partner(): return lax.ppermute(block, axis, route)  101 us
    all_to_all x2, waiting for transfers between devices, sum_at_owner(): lax.all_to_all(blocks, axis, split_axis=0, concat_axis=0, tiled=True)  46.7 us
    all_to_all x1, waiting for transfers between devices, local(): parts = lax.all_to_all(parts, 'tensor', split_axis=0, concat_axis=0)  37 us
    unnamed x20, local copies, waits for them, and re-layouts  25.8 us
    broadcast_in_dim x2, other arithmetic, local(): return (weight_now[None], moment_now[None], jnp.stack(grads_out))  17 us
    dot_general x2, matrix products, local(): lax.dot_general(gathered, slope_grad, (((0,), (0,)), ((), ())), preferred...  14.7 us
  transfers between devices with their start and end apart: 7, of which 4 were waited for; matrix products, arithmetic and copies ran while one was open for 9% of the time, Pallas kernels for 0%

profile of v1, /device:TPU:0, one launch (start us, length us, event | category | flops | bytes accessed | tf_op | source)
XLA Modules:
  0.0 518.0 jit_solution(17351530630381749916)
XLA Ops:
  0.6 1.7 slice_bitcast_fusion
  2.4 2.5 stack.15
  4.9 5.2 %all-to-all-start = ((bf16[4,128,4096]{2,1,0:T(8,128)(2,1)}), bf16[4,128,4096]{2,1,0:T(8,128)(2,1)}, u32[]{:S(2)}, u32[]{:S(2)}) async-start(bf16[4,128,4096]{2,1,0:T(8,128)(2,1)} %stack.15), calls=%async_computation | async-start | bytes 8388608 | tf_op jit(solution)/shard_map/all_to_all | solution.py:68
  10.1 6.5 %copy.8 = bf16[1,4096,512]{1,2,0:T(8,128)(2,1)} copy(bf16[1,4096,512]{2,1,0:T(8,128)(2,1)} %param.5) | data formatting | bytes 8388608 | tf_op args[1]
  16.6 6.3 %copy.7 = bf16[1,4096,512]{1,2,0:T(8,128)(2,1)} copy(bf16[1,4096,512]{2,1,0:T(8,128)(2,1)} %param.4) | data formatting | bytes 8388608 | tf_op args[0]
  22.9 37.0 %all-to-all-done = bf16[4,128,4096]{2,1,0:T(8,128)(2,1)} async-done(((bf16[4,128,4096]{2,1,0:T(8,128)(2,1)}), bf16[4,128,4096]{2,1,0:T(8,128)(2,1)}, u32[]{:S(2)}, u32[]{:S(2)}) %all-to-all-start) | async-done | bytes 4194336 | tf_op jit(solution)/shard_map/all_to_all | solution.py:68
  59.9 0.0 copy-start.1
  59.9 0.0 copy-start.2
  59.9 0.0 copy-start.7
  59.9 5.9 %fusion.13 = f32[512,512]{1,0:T(8,128)S(1)} fusion(bf16[512,4096]{1,0:T(8,128)(2,1)} %bitcast.4, bf16[1,4096,512]{2,1,0:T(8,128)(2,1)} %param.4), kind=kOutput, calls=%fused_computation.23 | convolution fusion | flops 2147483648 | bytes 9437184 | tf_op jit(solution)/shard_map/dot_general | solution.py:70
  65.8 0.0 copy-done.1
  65.8 0.0 copy-done.2
  65.8 0.2 copy-done.7
  66.0 6.5 %fusion.1 = (bf16[4096,512]{0,1:T(8,128)(2,1)S(1)}, bf16[4096,512]{0,1:T(8,128)(2,1)S(1)}) fusion(bf16[1,4096,512]{1,2,0:T(8,128)(2,1)S(1)} %copy-done.2, bf16[512,4096]{1,0:T(8,128)(2,1)} %bitcast.4, f32[512,512]{1,0:T(8,128)S(1)} %fusion.13, bf16[2,512,512]{2,1,0:T(8,128)(2,1)S(1)} %copy-done.7, bf16[1,4096,512]{1,2,0:T(8,128)(2,1)S(1)} %copy-done.1), kind=kOutput, calls=%fused_computation.5 | convolution fusion | flops 2168979456 | bytes 22544384 | tf_op jit(solution)/shard_map/dot_general | solution.py:72
  72.5 0.0 copy-start.3
  72.6 1.7 collective-permute-start
  74.2 0.4 collective-permute-start.1
  74.7 0.5 stack.16
  75.2 225.2 %all_to_all.20 = bf16[4,128,4096]{2,1,0:T(8,128)(2,1)S(1)} all-to-all(bf16[4,128,4096]{2,1,0:T(8,128)(2,1)S(1)} %stack.16), channel_id=1, replica_groups=mesh['replica'=32,'tensor'=4] {'tensor'}, dimensions={0} | all-to-all | bytes 8388608 | tf_op jit(solution)/shard_map/all_to_all | solution.py:68
  300.3 0.0 collective-permute-done
  300.3 0.0 copy-done.3
  300.4 2.4 convolution_bitcast_fusion
  302.8 0.0 copy-done.5
  302.8 0.0 copy-start
  302.8 0.0 collective-permute-done.1
  302.8 8.2 %fusion.8 = bf16[4096,512]{0,1:T(8,128)(2,1)} fusion(bf16[4096,512]{0,1:T(8,128)(2,1)} %collective-permute-done.1, bf16[4096,512]{0,1:T(8,128)(2,1)S(1)} %get-tuple-element.11, bf16[512,4096]{1,0:T(8,128)(2,1)S(1)} %bitcast.63, f32[512,512]{1,0:T(8,128)S(1)} %convolution_bitcast_fusion, bf16[2,512,512]{2,1,0:T(8,128)(2,1)S(1)} %copy-done.7), kind=kOutput, calls=%fused_computation.13 | convolution fusion | flops 2168979456 | bytes 18350080 | tf_op jit(solution)/shard_map/dot_general | solution.py:72
  311.0 1.5 collective-permute-start.3
  312.5 0.0 copy-done
  312.5 4.5 convolution_convert_fusion.1
  317.1 4.8 all-to-all-start.2
  321.9 0.0 copy-start.4
  321.9 0.0 copy-start.6
  321.9 81.4 %collective-permute-done.3 = bf16[4096,512]{0,1:T(8,128)(2,1)} collective-permute-done((bf16[4096,512]{0,1:T(8,128)(2,1)}, bf16[4096,512]{0,1:T(8,128)(2,1)}, u32[]{:S(2)}, u32[]{:S(2)}) %collective-permute-start.3) | collective-permute-done | bytes 4194336 | tf_op jit(solution)/shard_map/ppermute | solution.py:29
  403.3 9.8 %fusion.11 = (bf16[1,4096,512]{1,2,0:T(8,128)(2,1)}, bf16[4096,512]{0,1:T(8,128)(2,1)}) fusion(bf16[4096,512]{0,1:T(8,128)(2,1)} %collective-permute-done.3, bf16[4096,512]{0,1:T(8,128)(2,1)} %fusion.8, bf16[4096,512]{0,1:T(8,128)(2,1)} %copy-done.5, bf16[4096,512]{0,1:T(8,128)(2,1)} %copy-done.3), kind=kLoop, calls=%fused_computation.21 | loop fusion | flops 29360128 | bytes 25165824 | tf_op jit(solution)/shard_map/broadcast_in_dim | solution.py:79
  413.1 1.5 collective-permute-start.2
  414.6 0.0 copy-done.4
  414.6 0.0 copy-done.6
  414.6 4.8 convolution_convert_fusion
  419.4 0.0 all-to-all-done.2
  419.4 4.9 all-to-all-start.3
  424.3 3.1 reduce_sum.24
  427.3 46.7 %all-to-all-done.3 = bf16[4,128,4096]{2,1,0:T(8,128)(2,1)} async-done(((bf16[4,128,4096]{2,1,0:T(8,128)(2,1)}), bf16[4,128,4096]{2,1,0:T(8,128)(2,1)}, u32[]{:S(2)}, u32[]{:S(2)}) %all-to-all-start.3) | async-done | bytes 4194336 | tf_op jit(solution)/shard_map/all_to_all | solution.py:18
  474.0 3.1 reduce_sum.25
  477.1 1.5 pad_maximum_fusion
  478.6 6.4 %copy.11 = bf16[1,4096,512]{2,1,0:T(8,128)(2,1)} copy(bf16[1,4096,512]{1,2,0:T(8,128)(2,1)} %get-tuple-element.6) | data formatting | bytes 8388608
  485.0 19.5 %collective-permute-done.2 = bf16[4096,512]{0,1:T(8,128)(2,1)} collective-permute-done((bf16[4096,512]{0,1:T(8,128)(2,1)}, bf16[4096,512]{0,1:T(8,128)(2,1)}, u32[]{:S(2)}, u32[]{:S(2)}) %collective-permute-start.2) | collective-permute-done | bytes 4194336 | tf_op jit(solution)/shard_map/ppermute | solution.py:29
  504.5 7.2 %fusion.10 = bf16[1,4096,512]{1,2,0:T(8,128)(2,1)} fusion(bf16[4096,512]{0,1:T(8,128)(2,1)} %collective-permute-done.2, bf16[4096,512]{0,1:T(8,128)(2,1)} %get-tuple-element.7), kind=kLoop, calls=%fused_computation.20 | loop fusion | flops 10485760 | bytes 12582912 | tf_op jit(solution)/shard_map/broadcast_in_dim | solution.py:79
  511.6 6.4 %copy.10 = bf16[1,4096,512]{2,1,0:T(8,128)(2,1)} copy(bf16[1,4096,512]{1,2,0:T(8,128)(2,1)} %fusion.10) | data formatting | bytes 8388608
  (1 shorter events, 0.0 us)
Async XLA Ops:
  4.9 55.0 %all-to-all-start = ((bf16[4,128,4096]{2,1,0:T(8,128)(2,1)}), bf16[4,128,4096]{2,1,0:T(8,128)(2,1)}, u32[]{:S(2)}, u32[]{:S(2)}) async-start(bf16[4,128,4096]{2,1,0:T(8,128)(2,1)} %stack.15), calls=%async_computation | async-start | bytes 8388608 | tf_op jit(solution)/shard_map/all_to_all | solution.py:68
  59.9 5.9 %copy-start.1 = (bf16[1,4096,512]{1,2,0:T(8,128)(2,1)S(1)}, bf16[1,4096,512]{1,2,0:T(8,128)(2,1)}, u32[]{:S(2)}) copy-start(bf16[1,4096,512]{1,2,0:T(8,128)(2,1)} %copy.8) | copy-start | bytes 12582916
  59.9 5.9 %copy-start.2 = (bf16[1,4096,512]{1,2,0:T(8,128)(2,1)S(1)}, bf16[1,4096,512]{1,2,0:T(8,128)(2,1)}, u32[]{:S(2)}) copy-start(bf16[1,4096,512]{1,2,0:T(8,128)(2,1)} %copy.7) | copy-start | bytes 12582916
  59.9 6.1 %copy-start.7 = (bf16[2,512,512]{2,1,0:T(8,128)(2,1)S(1)}, bf16[2,512,512]{2,1,0:T(8,128)(2,1)}, u32[]{:S(2)}) copy-start(bf16[2,512,512]{2,1,0:T(8,128)(2,1)} %param.7) | copy-start | bytes 3145732
  72.5 227.8 %copy-start.3 = (bf16[4096,512]{0,1:T(8,128)(2,1)}, bf16[4096,512]{0,1:T(8,128)(2,1)S(1)}, u32[]{:S(2)}) copy-start(bf16[4096,512]{0,1:T(8,128)(2,1)S(1)} %get-tuple-element.10) | copy-start | bytes 12582916
  72.6 227.8 %collective-permute-start = (bf16[4096,512]{0,1:T(8,128)(2,1)S(1)}, bf16[4096,512]{0,1:T(8,128)(2,1)S(1)}, u32[]{:S(2)}, u32[]{:S(2)}) collective-permute-start(bf16[4096,512]{0,1:T(8,128)(2,1)S(1)} %get-tuple-element.10), channel_id=1, source_target_pairs={{0,4},{4,0},{8,12},{12,8},{16,20},{20,16},{24,28},{28,24},{32,36},... | collective-permute-start | bytes 12582920 | tf_op jit(solution)/shard_map/ppermute | solution.py:29
  74.2 228.6 %collective-permute-start.1 = (bf16[4096,512]{0,1:T(8,128)(2,1)S(1)}, bf16[4096,512]{0,1:T(8,128)(2,1)}, u32[]{:S(2)}, u32[]{:S(2)}) collective-permute-start(bf16[4096,512]{0,1:T(8,128)(2,1)S(1)} %get-tuple-element.11), channel_id=1, source_target_pairs={{0,4},{4,0},{8,12},{12,8},{16,20},{20,16},{24,28},{28,24},{32,36},... | collective-permute-start | bytes 12582920 | tf_op jit(solution)/shard_map/ppermute | solution.py:29
  300.3 2.5 copy-start.5
  302.8 9.7 %copy-start = (bf16[1,4096,512]{2,1,0:T(8,128)(2,1)S(1)}, bf16[1,4096,512]{2,1,0:T(8,128)(2,1)}, u32[]{:S(2)}) copy-start(bf16[1,4096,512]{2,1,0:T(8,128)(2,1)} %param.4) | copy-start | bytes 12582916
  311.0 92.2 %collective-permute-start.3 = (bf16[4096,512]{0,1:T(8,128)(2,1)}, bf16[4096,512]{0,1:T(8,128)(2,1)}, u32[]{:S(2)}, u32[]{:S(2)}) collective-permute-start(bf16[4096,512]{0,1:T(8,128)(2,1)} %fusion.8), channel_id=1, source_target_pairs={{0,8},{8,0},{4,12},{12,4},{16,24},{24,16},{20,28},{28,20},{32,40},... | collective-permute-start | bytes 12582920 | tf_op jit(solution)/shard_map/ppermute | solution.py:29
  317.1 102.4 %all-to-all-start.2 = ((bf16[4,128,4096]{2,1,0:T(8,128)(2,1)}), bf16[4,128,4096]{2,1,0:T(8,128)(2,1)}, u32[]{:S(2)}, u32[]{:S(2)}) async-start(bf16[4,128,4096]{2,1,0:T(8,128)(2,1)} %bitcast.60), calls=%async_computation.2 | async-start | bytes 8388608 | tf_op jit(solution)/shard_map/all_to_all | solution.py:18
  321.9 92.7 %copy-start.4 = (bf16[4096,512]{0,1:T(8,128)(2,1)S(1)}, bf16[4096,512]{0,1:T(8,128)(2,1)}, u32[]{:S(2)}) copy-start(bf16[4096,512]{0,1:T(8,128)(2,1)} %copy-done.3) | copy-start | bytes 12582916
  321.9 92.7 %copy-start.6 = (bf16[4096,512]{0,1:T(8,128)(2,1)S(1)}, bf16[4096,512]{0,1:T(8,128)(2,1)}, u32[]{:S(2)}) copy-start(bf16[4096,512]{0,1:T(8,128)(2,1)} %copy-done.5) | copy-start | bytes 12582916
  413.1 91.3 %collective-permute-start.2 = (bf16[4096,512]{0,1:T(8,128)(2,1)}, bf16[4096,512]{0,1:T(8,128)(2,1)}, u32[]{:S(2)}, u32[]{:S(2)}) collective-permute-start(bf16[4096,512]{0,1:T(8,128)(2,1)} %get-tuple-element.7), channel_id=1, source_target_pairs={{0,8},{8,0},{4,12},{12,4},{16,24},{24,16},{20,28},{28,20},{32,40},... | collective-permute-start | bytes 12582920 | tf_op jit(solution)/shard_map/ppermute | solution.py:29
  419.4 54.6 %all-to-all-start.3 = ((bf16[4,128,4096]{2,1,0:T(8,128)(2,1)}), bf16[4,128,4096]{2,1,0:T(8,128)(2,1)}, u32[]{:S(2)}, u32[]{:S(2)}) async-start(bf16[4,128,4096]{2,1,0:T(8,128)(2,1)} %bitcast.61), calls=%async_computation.3 | async-start | bytes 8388608 | tf_op jit(solution)/shard_map/all_to_all | solution.py:18
